TPU v7x, 512 devices: a whole 4x4x16 slice. The times are simulated.
512 devices in a mesh: pipe: 16 (over z), hid: 32 (over x, y, core).
Axes of the slice: x: 4, y: 4, z: 16, core: 2. Of those that a mesh axis runs over, the one named last changes fastest.
Arguments:
- section_inputs: bfloat16 [16, 3, 256, 1024], P('pipe', None, 'hid'), may hold values from -6 to 6
- w_in: bfloat16 [16, 1024, 32768], P('pipe', None, 'hid'), may hold values from -0.1875 to 0.1875
- w_out: bfloat16 [16, 32768, 1024], P('pipe', 'hid'), may hold values from -0.03125 to 0.03125
- warm_factor: float32 [16, 1024, 16], P('pipe'), may hold values from -6 to 6
- pending_left: float32 [16, 256, 16], P('pipe'), may hold values from -0.375 to 0.375
- pending_right: float32 [16, 1024, 16], P('pipe'), may hold values from -24 to 24
- incoming_left: float32 [3, 256, 16], replicated, may hold values from -0.375 to 0.375
- incoming_right: float32 [3, 1024, 16], replicated, may hold values from -24 to 24
Outputs:
- section_grads: float32 [16, 256, 1024], P('pipe', 'hid')
- final_left: float32 [16, 256, 16], P('pipe', 'hid')
- final_right: float32 [16, 1024, 16], P('pipe')
All inputs are finite; a program needn't handle non-finite values.
Results may differ from a plain program's by a relative error of at most 0.02.
Values may be sent and summed in bfloat16 or wider, within the bound.
A program may use at most 64 MiB of HBM per device.

v0:
```python
import jax
import jax.numpy as jnp
from jax import lax
from jax.sharding import PartitionSpec as P

TICKS = 3


def shifted(value, axis, steps):
    count = lax.axis_size(axis)
    leading, last = (max(0, -steps), min(count, count - steps))
    return lax.ppermute(value, axis, [(source, source + steps) for source in range(leading, last)])


def solve_lower(lower_factor, matrix):
    return jax.scipy.linalg.solve_triangular(lower_factor, matrix.T, lower=True).T


def high_dot(first, second):
    return jnp.dot(
        first, second, precision=lax.Precision.HIGHEST, preferred_element_type=jnp.float32
    )


def rows_product(first, second):
    return lax.dot_general(
        first,
        second,
        (((0,), (0,)), ((), ())),
        precision=lax.Precision.HIGHEST,
        preferred_element_type=jnp.float32,
    )


def body(
    section_inputs,
    w_in,
    w_out,
    warm_factor,
    pending_left,
    pending_right,
    incoming_left,
    incoming_right,
):
    w_in_section = w_in[0]
    w_out_section = w_out[0]
    is_top = lax.axis_index("pipe") == lax.axis_size("pipe") - 1
    rows_own = section_inputs.shape[2]
    lane_index = lax.axis_index("hid")
    row_offset = lane_index * rows_own
    held_left = pending_left[0]
    held_right = pending_right[0]
    warm_basis = warm_factor[0]
    merged_rows = None
    left_rows = None
    right_new = None
    for tick_index in range(TICKS):
        left_factor = jnp.where(is_top, incoming_left[tick_index], held_left)
        right_factor = jnp.where(is_top, incoming_right[tick_index], held_right)
        cotangent = lax.dot_general(
            left_factor,
            right_factor,
            (((1,), (1,)), ((), ())),
            precision=lax.Precision.HIGHEST,
            preferred_element_type=jnp.float32,
        )
        cotangent_low = cotangent.astype(jnp.bfloat16)
        upward = lax.dot_general(
            cotangent_low,
            w_out_section,
            (((1,), (1,)), ((), ())),
            preferred_element_type=jnp.float32,
        )
        preact = jnp.dot(
            lax.all_gather(section_inputs[0, tick_index], "hid", axis=0, tiled=True),
            w_in_section,
            preferred_element_type=jnp.float32,
        )
        hidden_grad = jnp.where(preact > 0, upward, jnp.zeros_like(upward)).astype(jnp.bfloat16)
        last_tick = tick_index + 1 == TICKS
        partial_value = lax.dot_general(
            hidden_grad, w_in_section, (((1,), (1,)), ((), ())), preferred_element_type=jnp.float32
        )
        summed = lax.psum(partial_value, "hid")
        merged = cotangent + summed
        projected = high_dot(merged, warm_basis)
        gram_matrix = rows_product(projected, projected)
        lower_factor = jnp.linalg.cholesky(gram_matrix)
        left_new = solve_lower(lower_factor, projected)
        right_new = rows_product(merged, left_new)
        merged_rows = lax.dynamic_slice_in_dim(merged, row_offset, rows_own, 0)
        left_rows = lax.dynamic_slice_in_dim(left_new, row_offset, rows_own, 0)
        if not last_tick:
            held_left, held_right = shifted((left_new, right_new), "pipe", -1)
        warm_basis = right_new
    return (merged_rows[None], left_rows[None], right_new[None])


def solution(mesh):
    placed = (
        P("pipe", None, "hid", None),
        P("pipe", None, "hid"),
        P("pipe", "hid", None),
        P("pipe", None, None),
        P("pipe", None, None),
        P("pipe", None, None),
        P(),
        P(),
    )
    return jax.shard_map(
        body,
        mesh=mesh,
        in_specs=placed,
        out_specs=(P("pipe", "hid", None), P("pipe", "hid", None), P("pipe", None, None)),
        check_vma=False,
    )
```

profile of v0, /device:TPU:1, one launch (start us, length us, event | category | flops | bytes accessed | tf_op | source)
XLA Modules:
  0.0 509.3 jit_solution(14217537990296651545)
XLA Ops:
  8.1 28.5 %all-gather = bf16[1,1,256,1024]{3,2,1,0:T(8,128)(2,1)S(1)} all-gather(bf16[1,1,8,1024]{3,2,1,0:T(8,128)(2,1)S(1)} %get-tuple-element.6), channel_id=2, replica_groups=mesh['pipe'=16,'hid'=32] {'hid'}, dimensions={2}, use_global_device_ids=true | all-gather | bytes 540672 | tf_op jit(solution)/shard_map/all_gather | solution.py:75
  36.6 1.4 fusion.36
  39.1 4.3 fusion.14
  43.5 27.1 %all-gather.1 = bf16[1,1,256,1024]{3,2,1,0:T(8,128)(2,1)} all-gather(bf16[1,1,8,1024]{3,2,1,0:T(8,128)(2,1)S(1)} %get-tuple-element.7), channel_id=3, replica_groups=mesh['pipe'=16,'hid'=32] {'hid'}, dimensions={2}, use_global_device_ids=true | all-gather | bytes 540672 | tf_op jit(solution)/shard_map/all_gather | solution.py:75
  70.6 108.9 %all-reduce.4.cloned.1.call-done = f32[256,1024]{1,0:T(8,128)} async-done(((f32[256,1024]{1,0:T(8,128)}), f32[256,1024]{1,0:T(8,128)}) %all-reduce.4.cloned.1.call-update) | async-done | bytes 1048592 | tf_op jit(solution)/shard_map/psum | solution.py:84
  179.4 1.7 add.28
  182.3 1.5 cholesky.59
  187.2 1.3 collective-permute-start.1
  188.5 1.3 collective-permute-start
  189.8 2.5 fusion.39
  192.3 1.4 collective-permute-done
  194.7 4.3 fusion.10
  199.0 29.3 %all-gather.2 = bf16[1,1,256,1024]{3,2,1,0:T(8,128)(2,1)} all-gather(bf16[1,1,8,1024]{3,2,1,0:T(8,128)(2,1)S(1)} %get-tuple-element.5), channel_id=4, replica_groups=mesh['pipe'=16,'hid'=32] {'hid'}, dimensions={2}, use_global_device_ids=true | all-gather | bytes 540672 | tf_op jit(solution)/shard_map/all_gather | solution.py:75
  228.4 107.9 %all-reduce.6.cloned.1.call-done = f32[256,1024]{1,0:T(8,128)} async-done(((f32[256,1024]{1,0:T(8,128)}), f32[256,1024]{1,0:T(8,128)}) %all-reduce.6.cloned.1.call-update) | async-done | bytes 1048592 | tf_op jit(solution)/shard_map/psum | solution.py:84
  336.3 1.7 add.29
  339.1 1.5 cholesky.70
  345.3 1.3 collective-permute-start.2
  346.6 2.5 fusion.42
  349.1 1.4 collective-permute-done.2
  351.6 4.3 fusion.6
  355.9 137.2 %all-reduce.8.cloned.1.call-done = f32[256,1024]{1,0:T(8,128)} async-done(((f32[256,1024]{1,0:T(8,128)}), f32[256,1024]{1,0:T(8,128)}) %all-reduce.8.cloned.1.call-update) | async-done | bytes 1048592 | tf_op jit(solution)/shard_map/psum | solution.py:84
  493.1 1.7 add.30
  495.9 1.5 cholesky.81
  500.2 1.3 convolution_bitcast_fusion
  (63 shorter events, 19.9 us)
Async XLA Ops:
  7.2 29.4 %copy-start = (bf16[1,1024,1024]{2,1,0:T(8,128)(2,1)S(1)}, bf16[1,1024,1024]{2,1,0:T(8,128)(2,1)}, u32[]{:S(2)}) copy-start(bf16[1,1024,1024]{2,1,0:T(8,128)(2,1)} %param.12) | copy-start | bytes 6291460
  7.2 172.3 %all-reduce.4.cloned.1.call-start = ((), (), s32[]{:S(2)}) async-start(), calls=%async_computation | async-start | bytes 2097152 | tf_op jit(solution)/shard_map/psum | solution.py:84
  36.6 1.5 copy-start.4
  36.6 1.5 copy-start.5
  36.6 1.5 copy-start.7
  36.6 1.5 copy-start.8
  39.1 4.3 copy-start.3
  43.4 137.7 %copy-start.6 = (f32[1,1024,16]{1,2,0:T(8,128)S(1)}, f32[1,1024,16]{1,2,0:T(8,128)}, u32[]{:S(2)}) copy-start(f32[1,1024,16]{1,2,0:T(8,128)} %param.14) | copy-start | bytes 196612
  43.4 292.9 %all-reduce.6.cloned.1.call-start = ((), (), s32[]{:S(2)}) async-start(), calls=%async_computation.1 | async-start | bytes 2097152 | tf_op jit(solution)/shard_map/psum | solution.py:84
  187.2 6.5 %collective-permute-start.1 = (f32[1024,16]{0,1:T(8,128)S(1)}, f32[1024,16]{0,1:T(8,128)S(1)}, u32[]{:S(2)}, u32[]{:S(2)}) collective-permute-start(f32[1024,16]{0,1:T(8,128)S(1)} %fusion.106), channel_id=1, source_target_pairs={{32,0},{64,32},{96,64},{128,96},{160,128},{192,160},{224,192},{256... | collective-permute-start | bytes 196616 | tf_op jit(solution)/shard_map/ppermute | solution.py:12
  188.5 5.2 %collective-permute-start = (f32[256,16]{0,1:T(8,128)S(1)}, f32[256,16]{0,1:T(8,128)S(1)}, u32[]{:S(2)}, u32[]{:S(2)}) collective-permute-start(f32[256,16]{0,1:T(8,128)S(1)} %bitcast.136), channel_id=1, source_target_pairs={{32,0},{64,32},{96,64},{128,96},{160,128},{192,160},{224,192},{256... | collective-permute-start | bytes 49160 | tf_op jit(solution)/shard_map/ppermute | solution.py:12
  194.7 4.3 copy-start.2
  199.0 294.1 %all-reduce.8.cloned.1.call-start = ((), (), s32[]{:S(2)}) async-start(), calls=%async_computation.2 | async-start | bytes 2097152 | tf_op jit(solution)/shard_map/psum | solution.py:84
  344.0 6.5 %collective-permute-start.3 = (f32[1024,16]{0,1:T(8,128)S(1)}, f32[1024,16]{0,1:T(8,128)S(1)}, u32[]{:S(2)}, u32[]{:S(2)}) collective-permute-start(f32[1024,16]{0,1:T(8,128)S(1)} %fusion.109), channel_id=1, source_target_pairs={{32,0},{64,32},{96,64},{128,96},{160,128},{192,160},{224,192},{256... | collective-permute-start | bytes 196616 | tf_op jit(solution)/shard_map/ppermute | solution.py:12
  345.3 5.2 %collective-permute-start.2 = (f32[256,16]{0,1:T(8,128)S(1)}, f32[256,16]{0,1:T(8,128)S(1)}, u32[]{:S(2)}, u32[]{:S(2)}) collective-permute-start(f32[256,16]{0,1:T(8,128)S(1)} %bitcast.137), channel_id=1, source_target_pairs={{32,0},{64,32},{96,64},{128,96},{160,128},{192,160},{224,192},{256... | collective-permute-start | bytes 49160 | tf_op jit(solution)/shard_map/ppermute | solution.py:12
  351.6 4.3 copy-start.1
Sparse Core Ops, SparseCore 0:
  43.5 135.8 all-reduce.3
  199.1 137.1 all-reduce.5
  356.0 137.0 all-reduce.7
where the time goes:
time: 510 us; the launch traced here: 509 us
  waiting for transfers between devices  357 us (70%)
  blocking collectives  84.9 us (17%)
  matrix products  28.7 us (6%)
  other arithmetic  17.1 us (3%)
  between operations  13.9 us (3%)
  starting transfers between devices  5.28 us (1%)
    psum x3, waiting for transfers between devices, body(): summed = lax.psum(partial_value, 'hid')  354 us
    all_gather x3, blocking collectives, body(): lax.all_gather(section_inputs[0, tick_index], 'hid', axis=0, tiled=True)  84.9 us
    dot_general x3, matrix products, body(): lax.dot_general(hidden_grad, w_in_section, (((1,), (1,)), ((), ())), pref...  12.8 us
  transfers between devices with their start and end apart: 7, of which 5 were waited for; matrix products, arithmetic and copies ran while one was open for 1% of the time, Pallas kernels for 0%

commit v1 on v0

v1 whole, which is shorter than its diff:
```python
import jax
import jax.numpy as jnp
from jax import lax
from jax.experimental import pallas as pl
from jax.experimental.pallas import tpu as pltpu
from jax.sharding import PartitionSpec as P

MESH = pl.DeviceIdType.MESH
F32 = jnp.float32
BF16 = jnp.bfloat16
TICKS = 3
NX, NY, NC = 4, 4, 2
CHIPS = NX * NY
RANK = 16
ROWS = 256
D = 1024
LANES = 128
PIECES = D // LANES
OWN = ROWS // (CHIPS * NC)


def split(value):
    high = value.astype(BF16)
    low = (value - high.astype(F32)).astype(BF16)
    return high, low


def mm(first, second, dims=((1,), (0,))):
    return lax.dot_general(first, second, (dims, ((), ())), preferred_element_type=F32)


def mm_high(first, second, dims=((1,), (0,))):
    return lax.dot_general(
        first,
        second,
        (dims, ((), ())),
        precision=lax.Precision.HIGHEST,
        preferred_element_type=F32,
    )


def thin(value, matrix, dims):
    high, low = split(value)
    both = mm(jnp.concatenate([high, low], axis=0), matrix, dims)
    return both[:RANK] + both[RANK:]


def inverse_lower(gram):
    row = lax.broadcasted_iota(jnp.int32, (RANK, LANES), 0)
    lane = lax.broadcasted_iota(jnp.int32, (RANK, LANES), 1)
    work = jnp.concatenate([gram, jnp.zeros((RANK, LANES - RANK), F32)], axis=1)
    work = work + jnp.where(lane == row + RANK, 1.0, 0.0).astype(F32)
    pivots = jnp.zeros((RANK, LANES), F32)
    for k in range(RANK):
        column = jnp.broadcast_to(work[:, k : k + 1], (RANK, LANES))
        pivot = jnp.broadcast_to(column[k : k + 1, :], (RANK, LANES))
        along = jnp.broadcast_to(work[k : k + 1, :], (RANK, LANES))
        factor = jnp.where(row > k, column / pivot, 0.0)
        work = work - factor * along
        pivots = jnp.where(row == k, pivot, pivots)
    scaled = work * lax.rsqrt(pivots)
    return scaled[:, RANK : 2 * RANK]


def kernel(
    x_hbm,
    wi_hbm,
    wo_hbm,
    warm_hbm,
    pend_l_hbm,
    pend_r_hbm,
    inc_l_hbm,
    inc_r_hbm,
    grads_out,
    left_out,
    right_out,
    wi,
    wo,
    x_full,
    mask,
    hg,
    l_f32,
    r_f32,
    b_f32,
    l_inc,
    r_inc,
    ps,
    pbuf1,
    ps1,
    pbuf2,
    zs,
    zbuf1,
    zs1,
    zbuf2,
    rp,
    rbuf,
    rzbuf,
    ls,
    lz,
    rows_f32,
    mfull,
    msend,
    mpair,
    mpart,
    mbuf,
    local_sem,
    ag_send,
    ag_recv,
    agp_send,
    agp_recv,
    p1_send,
    p1_recv,
    p2_send,
    p2_recv,
    z1_send,
    z1_recv,
    z2_send,
    z2_recv,
    r_send,
    r_recv,
    rz_send,
    rz_recv,
    l_send,
    l_recv,
    m_send,
    m_recv,
):
    s = lax.axis_index("pipe")
    last_section = lax.axis_size("pipe") - 1
    h = lax.axis_index("hid")
    chip = h // NC
    c = h % NC
    x = chip // NY
    y = chip % NY
    oc = 1 - c
    xs = [x] + [(x + o) % NX for o in range(1, NX)]
    ys = [y] + [(y + o) % NY for o in range(1, NY)]
    cs = [c, oc]
    g1 = x * NC + c
    is_top = s == last_section
    has_above = s < last_section
    has_below = s > 0
    far = (2, 1, 3)
    group = [(o, e) for o in far for e in range(NC)] + [(0, 1)]
    chips = [(i, j) for i in (2, 1, 3, 0) for j in (2, 1, 3, 0) if (i, j) != (0, 0)]

    def hid(xx, yy, cc):
        return xx * (NY * NC) + yy * NC + cc

    def send(src, dst, send_sem, recv_sem, target):
        pltpu.make_async_remote_copy(
            src_ref=src,
            dst_ref=dst,
            send_sem=send_sem,
            recv_sem=recv_sem,
            device_id=target,
            device_id_type=MESH,
        ).start()

    def drain(ref, sem, name="out"):
        with jax.named_scope(name):
            pltpu.make_async_copy(ref, ref, sem).wait()

    barrier = pltpu.get_barrier_semaphore()

    def signal(target):
        pl.semaphore_signal(barrier, inc=1, device_id=target, device_id_type=MESH)

    for i, j in chips:
        signal((s, hid(xs[i], ys[j], c)))

    @pl.when(has_below)
    def _():
        for i in range(NX):
            for e in range(NC):
                signal((s - 1, hid(xs[i], y, cs[e])))

    @pl.when(has_above)
    def _():
        for i in range(NX):
            for e in range(NC):
                signal((s + 1, hid(xs[i], y, cs[e])))

    for o in far:
        signal((s, hid(xs[o], y, oc)))
        signal((s, hid(x, ys[o], oc)))
    signal((s, hid(x, y, oc)))

    own_x = [
        pltpu.make_async_copy(x_hbm.at[t], x_full.at[t, chip, c], ag_recv.at[t, 0])
        for t in range(TICKS)
    ]
    for copy in own_x:
        copy.start()
    loads = [
        pltpu.make_async_copy(warm_hbm, b_f32, local_sem.at[0]),
        pltpu.make_async_copy(inc_l_hbm, l_inc, local_sem.at[3]),
        pltpu.make_async_copy(inc_r_hbm, r_inc, local_sem.at[4]),
        pltpu.make_async_copy(pend_l_hbm, l_f32, local_sem.at[5]),
        pltpu.make_async_copy(pend_r_hbm, r_f32, local_sem.at[6]),
        pltpu.make_async_copy(wo_hbm, wo, local_sem.at[1]),
        pltpu.make_async_copy(wi_hbm, wi, local_sem.at[2]),
    ]
    for load in loads:
        load.start()

    neighbours = has_below.astype(jnp.int32) + has_above.astype(jnp.int32)
    with jax.named_scope("entry"):
        pl.semaphore_wait(barrier, CHIPS + 2 * (NX - 1) + NX * NC * neighbours)

    def gather_rows(t, targets):
        for i, j in targets:
            send(
                x_hbm.at[t],
                x_full.at[t, chip, c],
                ag_send.at[t],
                ag_recv.at[t, (NX - i) % NX],
                (s, hid(xs[i], ys[j], c)),
            )

    def share_rows(t):
        for i in (0, 1, 3, 2):
            four = x_full.at[t, pl.ds(xs[i] * NY, NY), c]
            drain(four, ag_recv.at[t, i], "ag_recv")
            send(four, four, agp_send.at[t], agp_recv.at[t], (s, hid(x, y, oc)))

    def make_mask(t):
        drain(x_full.at[t, :, oc], agp_recv.at[t], "agp_recv")
        with jax.named_scope("mask"):
            rows = x_full[t].reshape(ROWS, D)
            preact = mm(rows, wi[...])
            mask[...] = jnp.where(preact > 0, 1.0, 0.0).astype(BF16)

    def scatter_merged(targets):
        for i, j in targets:
            send(
                mpart.at[xs[i] * NY + ys[j]],
                mbuf.at[chip],
                m_send.at[1],
                m_recv.at[1],
                (s, hid(xs[i], ys[j], c)),
            )

    def low_cotangent():
        l_high, l_low = split(l_f32[...])
        r_high, r_low = split(r_f32[...])
        l_three = jnp.concatenate([l_high, l_high, l_low], axis=0)
        r_three = jnp.concatenate([r_high, r_low, r_high], axis=0)
        return mm(l_three, r_three, ((0,), (0,))).astype(BF16)

    gather_rows(0, chips)
    with jax.named_scope("loads"):
        for load in loads:
            load.wait()

    @pl.when(is_top)
    def _():
        l_f32[...] = l_inc[0]
        r_f32[...] = r_inc[0]

    for t in range(TICKS):
        last = t + 1 == TICKS
        if t > 0:
            drain(rbuf.at[t - 1, pl.ds(0, NX * NC - 1)], r_recv.at[t - 1], "r_recv")
            for j in range(PIECES):
                b_f32[:, j * LANES : (j + 1) * LANES] = rbuf[t - 1, j]
        with jax.named_scope("v"):
            v = thin(b_f32[...], wi[...], ((1,), (0,)))
        if t > 0:

            @pl.when(has_above)
            def _():
                drain(lz.at[t - 1], l_recv.at[t - 1], "l_recv")
                l_f32[...] = lz[t - 1]
                drain(rzbuf.at[t - 1], rz_recv.at[t - 1], "rz_recv")
                for j in range(PIECES):
                    r_f32[:, j * LANES : (j + 1) * LANES] = rzbuf[t - 1, j]

            @pl.when(is_top)
            def _():
                l_f32[...] = l_inc[t]
                r_f32[...] = r_inc[t]

        with jax.named_scope("upward"):
            upward = mm(low_cotangent(), wo[...], ((1,), (1,)))
            if t > 0:
                hg[...] = upward.astype(BF16) * mask[...]
            else:
                hg[...] = upward.astype(BF16)
        if t == 0:
            share_rows(0)
            make_mask(0)
            hg[...] = hg[...] * mask[...]
        with jax.named_scope("p_part"):
            p_part = thin(v, hg[...], ((1,), (1,)))
            ps[t, 0] = p_part[:, :LANES]
            ps[t, 1] = p_part[:, LANES:]
        for o, e in group:
            send(
                ps.at[t, cs[e]],
                pbuf1.at[t, g1],
                p1_send.at[t],
                p1_recv.at[t],
                (s, hid(xs[o], y, cs[e])),
            )
        pbuf1[t, g1] = ps[t, c]
        if not last:
            gather_rows(t + 1, chips[:5])
        with jax.named_scope("p_cot"):
            cross = mm_high(b_f32[...], r_f32[...], ((1,), (1,)))
            p_cot = mm_high(cross, l_f32[...])
        if last:
            with jax.named_scope("merged"):
                mfull[...] = mm(hg[...], wi[...], ((1,), (1,)))
                for k in range(CHIPS):
                    for e in range(NC):
                        base = (k * NC + e) * OWN
                        msend[e, k] = mfull[base : base + OWN, :].astype(BF16)
            send(
                msend.at[oc],
                mpair,
                m_send.at[0],
                m_recv.at[0],
                (s, hid(x, y, oc)),
            )
        drain(pbuf1.at[t, pl.ds(0, NX * NC - 1)], p1_recv.at[t], "p1_recv")
        p_sum = pbuf1[t, 0]
        for j in range(1, NX * NC):
            p_sum = p_sum + pbuf1[t, j]
        ps1[t] = p_sum
        for o, e in group:
            send(
                ps1.at[t],
                pbuf2.at[t, c * NY + y],
                p2_send.at[t],
                p2_recv.at[t],
                (s, hid(x, ys[o], cs[e])),
            )
        pbuf2[t, c * NY + y] = p_sum
        if last:
            drain(mpair, m_recv.at[0], "m_recv")
            with jax.named_scope("mpart"):
                mpart[...] = (msend[c].astype(F32) + mpair[...].astype(F32)).astype(BF16)
            scatter_merged(chips[:5])
            mbuf[chip] = mpart[chip]
        else:
            gather_rows(t + 1, chips[5:10])
        drain(pbuf2.at[t, pl.ds(0, NY * NC - 1)], p2_recv.at[t], "p2_recv")
        with jax.named_scope("z_part"):
            halves = []
            for e in range(NC):
                half = pbuf2[t, e * NY]
                for j in range(1, NY):
                    half = half + pbuf2[t, e * NY + j]
                halves.append(half)
            projected = jnp.concatenate(halves, axis=1) + p_cot
            y_part = thin(projected, hg[...], ((1,), (0,)))
            z_part = thin(y_part, wi[...], ((1,), (1,)))
            for j in range(PIECES):
                zs[t, j] = z_part[:, j * LANES : (j + 1) * LANES]
        for o, e in group:
            j = xs[o] * NC + cs[e]
            send(
                zs.at[t, j],
                zbuf1.at[t, g1],
                z1_send.at[t],
                z1_recv.at[t],
                (s, hid(xs[o], y, cs[e])),
            )
        zbuf1[t, g1] = zs[t, g1]
        if last:
            scatter_merged(chips[5:10])
        else:
            gather_rows(t + 1, chips[10:])
        with jax.named_scope("inverse"):
            gram = mm_high(projected, projected, ((1,), (1,)))
            inverse = inverse_lower(gram)
            new_left = mm_high(inverse, projected)
            if last:
                rows_f32[...] = new_left.T
                left_out[...] = rows_f32[pl.ds(pl.multiple_of(h * OWN, OWN), OWN), :]
            else:
                ls[t] = new_left
        if not last:

            @pl.when(has_below)
            def _():
                send(ls.at[t], lz.at[t], l_send.at[t], l_recv.at[t], (s - 1, h))

        with jax.named_scope("z_cot"):
            mix = mm_high(projected, l_f32[...], ((1,), (1,)))
            z_cot = mm_high(mix, r_f32[:, pl.ds(pl.multiple_of(g1 * LANES, LANES), LANES)])
        drain(zbuf1.at[t, pl.ds(0, NX * NC - 1)], z1_recv.at[t], "z1_recv")
        z_sum = zbuf1[t, 0]
        for j in range(1, NX * NC):
            z_sum = z_sum + zbuf1[t, j]
        zs1[t] = z_sum
        for o in far:
            send(
                zs1.at[t],
                zbuf2.at[t, y],
                z2_send.at[t],
                z2_recv.at[t],
                (s, hid(x, ys[o], c)),
            )
        zbuf2[t, y] = z_sum
        if not last:
            share_rows(t + 1)
            make_mask(t + 1)
        else:
            scatter_merged(chips[10:])
            with jax.named_scope("cot_rows"):
                rows_f32[...] = l_f32[...].T
                own_left = rows_f32[pl.ds(pl.multiple_of(h * OWN, OWN), OWN), :]
                merged = mm_high(own_left, r_f32[...])
        drain(zbuf2.at[t, pl.ds(0, NY - 1)], z2_recv.at[t], "z2_recv")
        with jax.named_scope("r_piece"):
            z_piece = z_cot
            for j in range(NY):
                z_piece = z_piece + zbuf2[t, j]
            r_piece = mm_high(inverse, z_piece)
            rp[t] = r_piece
        if not last:

            @pl.when(has_below)
            def _():
                for i in (2, 1, 3, 0):
                    for e in range(NC):
                        send(
                            rp.at[t],
                            rzbuf.at[t, g1],
                            rz_send.at[t],
                            rz_recv.at[t],
                            (s - 1, hid(xs[i], y, cs[e])),
                        )

        for o, e in group:
            send(
                rp.at[t],
                rbuf.at[t, g1],
                r_send.at[t],
                r_recv.at[t],
                (s, hid(xs[o], y, cs[e])),
            )
        rbuf[t, g1] = r_piece

    t = TICKS - 1
    drain(mbuf.at[pl.ds(0, CHIPS - 1)], m_recv.at[1], "m_recv")
    for k in range(CHIPS):
        merged = merged + mbuf[k].astype(F32)
    grads_out[...] = merged
    drain(rbuf.at[t, pl.ds(0, NX * NC - 1)], r_recv.at[t], "r_recv")
    for j in range(PIECES):
        right_out[:, j * LANES : (j + 1) * LANES] = rbuf[t, j]

    drain(msend.at[0], m_send.at[0])
    drain(mbuf.at[pl.ds(0, CHIPS - 1)], m_send.at[1])
    for t in range(TICKS):
        drain(x_full.at[t, pl.ds(0, CHIPS - 1), 0], ag_send.at[t])
        drain(x_full.at[t, :, 0], agp_send.at[t])
        drain(pbuf1.at[t, pl.ds(0, NX * NC - 1)], p1_send.at[t])
        drain(pbuf2.at[t, pl.ds(0, NY * NC - 1)], p2_send.at[t])
        drain(zbuf1.at[t, pl.ds(0, NX * NC - 1)], z1_send.at[t])
        drain(zbuf2.at[t, pl.ds(0, NY - 1)], z2_send.at[t])
        drain(rbuf.at[t, pl.ds(0, NX * NC - 1)], r_send.at[t])
        if t + 1 < TICKS:

            @pl.when(has_below)
            def _():
                drain(rzbuf.at[t], rz_send.at[t])
                drain(lz.at[t], l_send.at[t])


def hand_over(merged_in, left_in, right_in, merged_out, left_out, right_out):
    merged_out[...] = merged_in[...]
    left_out[...] = left_in[...]
    right_out[...] = right_in[...]


def body(
    section_inputs,
    w_in,
    w_out,
    warm_factor,
    pending_left,
    pending_right,
    incoming_left,
    incoming_right,
):
    width = w_in.shape[2]
    group = NX * NC
    dma = pltpu.SemaphoreType.DMA
    anywhere = pl.BlockSpec(memory_space=pltpu.MemorySpace.HBM)
    inside = pl.BlockSpec(memory_space=pltpu.VMEM)
    results = (
        jax.ShapeDtypeStruct((OWN, D), F32),
        jax.ShapeDtypeStruct((OWN, RANK), F32),
        jax.ShapeDtypeStruct((RANK, D), F32),
    )
    found = pl.pallas_call(
        kernel,
        out_shape=results,
        in_specs=[anywhere] * 8,
        out_specs=(inside, inside, inside),
        scratch_shapes=[
            pltpu.VMEM((D, width), BF16),
            pltpu.VMEM((width, D), BF16),
            pltpu.VMEM((TICKS, CHIPS, NC, OWN, D), BF16),
            pltpu.VMEM((ROWS, width), BF16),
            pltpu.VMEM((ROWS, width), BF16),
            pltpu.VMEM((RANK, ROWS), F32),
            pltpu.VMEM((RANK, D), F32),
            pltpu.VMEM((RANK, D), F32),
            pltpu.VMEM((TICKS, RANK, ROWS), F32),
            pltpu.VMEM((TICKS, RANK, D), F32),
            pltpu.VMEM((TICKS, NC, RANK, LANES), F32),
            pltpu.VMEM((TICKS, group, RANK, LANES), F32),
            pltpu.VMEM((TICKS, RANK, LANES), F32),
            pltpu.VMEM((TICKS, NC * NY, RANK, LANES), F32),
            pltpu.VMEM((TICKS, PIECES, RANK, LANES), F32),
            pltpu.VMEM((TICKS, group, RANK, LANES), F32),
            pltpu.VMEM((TICKS, RANK, LANES), F32),
            pltpu.VMEM((TICKS, NY, RANK, LANES), F32),
            pltpu.VMEM((TICKS, RANK, LANES), F32),
            pltpu.VMEM((TICKS, group, RANK, LANES), F32),
            pltpu.VMEM((TICKS, group, RANK, LANES), F32),
            pltpu.VMEM((TICKS, RANK, ROWS), F32),
            pltpu.VMEM((TICKS, RANK, ROWS), F32),
            pltpu.VMEM((ROWS, RANK), F32),
            pltpu.VMEM((ROWS, D), F32),
            pltpu.VMEM((NC, CHIPS, OWN, D), BF16),
            pltpu.VMEM((CHIPS, OWN, D), BF16),
            pltpu.VMEM((CHIPS, OWN, D), BF16),
            pltpu.VMEM((CHIPS, OWN, D), BF16),
            dma((7,)),
        ]
        + [dma((TICKS,)), dma((TICKS, NX))]
        + [dma((TICKS,))] * 16
        + [dma((2,))] * 2,
        compiler_params=pltpu.CompilerParams(
            collective_id=0, has_side_effects=True, vmem_limit_bytes=67043328
        ),
    )(
        section_inputs[0],
        w_in[0],
        w_out[0],
        jnp.swapaxes(warm_factor[0], 0, 1),
        jnp.swapaxes(pending_left[0], 0, 1),
        jnp.swapaxes(pending_right[0], 0, 1),
        jnp.swapaxes(incoming_left, 1, 2),
        jnp.swapaxes(incoming_right, 1, 2),
    )
    merged, left, right = pl.pallas_call(
        hand_over, out_shape=results, in_specs=[inside] * 3, out_specs=(inside,) * 3
    )(*found)
    return (merged[None], left[None], jnp.swapaxes(right, 0, 1)[None])


def solution(mesh):
    placed = (
        P("pipe", None, "hid", None),
        P("pipe", None, "hid"),
        P("pipe", "hid", None),
        P("pipe", None, None),
        P("pipe", None, None),
        P("pipe", None, None),
        P(),
        P(),
    )
    return jax.shard_map(
        body,
        mesh=mesh,
        in_specs=placed,
        out_specs=(P("pipe", "hid", None), P("pipe", "hid", None), P("pipe", None, None)),
        check_vma=False,
    )
```

time: 510 us -> 86.9 us (0.17)
  waiting for transfers between devices: 357 us -> 0 us
  Pallas kernels: 0 us -> 86 us
  blocking collectives: 84.9 us -> 0 us
  matrix products: 28.7 us -> 0 us
  other arithmetic: 17.1 us -> 0 us
  between operations: 13.9 us -> 0.64 us
  starting transfers between devices: 5.28 us -> 0 us
    psum x3 -> x0, waiting for transfers between devices: 354 us -> none  [body(): summed = lax.psum(partial_value, 'hid')]
    pallas_call x0 -> x2, Pallas kernels: none -> 86 us  [the longest x1 84.5 us: body(): pl.pallas_call(kernel, out_shape=results, in_specs=[anywhere] * 8, out_sp...]
    all_gather x3 -> x0, blocking collectives: 84.9 us -> none  [body(): lax.all_gather(section_inputs[0, tick_index], 'hid', axis=0, tiled=True)]
    dot_general x18 -> x0, matrix products: 28.1 us -> none  [the longest x3 12.8 us: body(): lax.dot_general(hidden_grad, w_in_section, (((1,), (1,)), ((), ())), pref...]
    another operation x15 -> x0, other arithmetic: 12.1 us -> none  [the longest x9 6.42 us: body(): lower_factor = jnp.linalg.cholesky(gram_matrix)]
    ppermute x4 -> x0, starting transfers between devices: 5.16 us -> none  [shifted(): lax.ppermute(value, axis, [(source, source + steps) for source in range(l...]
  transfers between devices with their start and end apart: 7 -> 0, of which waited for: 5 -> 0; matrix products, arithmetic and copies ran while one was open for 1% -> 0% of each run, Pallas kernels for 0% -> 0%
where the time goes in v1:
time: 86.9 us; the launch traced here: 86.6 us
  Pallas kernels  86 us (99%)
    pallas_call x1, Pallas kernels, body(): pl.pallas_call(kernel, out_shape=results, in_specs=[anywhere] * 8, out_sp...  84.5 us

profile of v1, /device:TPU:1, one launch (start us, length us, event | category | flops | bytes accessed | tf_op | source)
XLA Modules:
  0.0 86.6 jit_solution(7513207973847416381)
XLA Ops:
  0.6 84.5 %shard_map.103 = (f32[8,1024]{1,0:T(8,128)}, f32[8,16]{1,0:T(8,128)}, f32[16,1024]{1,0:T(8,128)}) custom-call(bf16[3,8,1024]{2,1,0:T(8,128)(2,1)} %bitcast.24, bf16[1024,1024]{1,0:T(8,128)(2,1)} %bitcast.19, bf16[1024,1024]{1,0:T(8,128)(2,1)} %bitcast.20, f32[16,1024]{1,0:T(8,128)} %bitcast.22, f32[16,256]{1,0:T(8,128)} %bitcast.26, f32[16,1024]{1,0:T(8,128)} %bitcast.23, ...), custom_call_target="tpu_custom_call" | custom-call | tf_op jit(solution)/shard_map/pallas_call | solution.py:500
  85.1 1.5 %shard_map.104 = (f32[8,1024]{1,0:T(8,128)}, f32[8,16]{1,0:T(8,128)}, f32[16,1024]{1,0:T(8,128)}) custom-call(f32[8,1024]{1,0:T(8,128)} %get-tuple-element.9.merged_in, f32[8,16]{1,0:T(8,128)} %get-tuple-element.10.left_in, f32[16,1024]{1,0:T(8,128)} %get-tuple-element.11.right_in), custom_call_target="tpu_custom_call" | custom-call | tf_op jit(solution)/shard_map/pallas_call | solution.py:553

commit v2 on v1

--- a/solution.py
+++ b/solution.py
@@ -17,6 +17,8 @@
 LANES = 128
 PIECES = D // LANES
 OWN = ROWS // (CHIPS * NC)
+HALF = RANK // 2
+GROUP = NX * NC
 
 
 def split(value):
@@ -43,6 +45,15 @@
     high, low = split(value)
     both = mm(jnp.concatenate([high, low], axis=0), matrix, dims)
     return both[:RANK] + both[RANK:]
+
+
+def times(inverse, value):
+    first_high, first_low = split(inverse)
+    high, low = split(value)
+    return mm(
+        jnp.concatenate([first_high, first_high, first_low], axis=1),
+        jnp.concatenate([high, low, high], axis=0),
+    )
 
 
 def inverse_lower(gram):
@@ -92,7 +103,12 @@
     zbuf1,
     zs1,
     zbuf2,
-    rp,
+    zc,
+    zp,
+    z_full,
+    a_f32,
+    m_high,
+    m_low,
     rbuf,
     rzbuf,
     ls,
@@ -137,6 +153,7 @@
     ys = [y] + [(y + o) % NY for o in range(1, NY)]
     cs = [c, oc]
     g1 = x * NC + c
+    g2 = y * NC + c
     is_top = s == last_section
     has_above = s < last_section
     has_below = s > 0
@@ -171,15 +188,19 @@
 
     @pl.when(has_below)
     def _():
-        for i in range(NX):
-            for e in range(NC):
+        for e in range(NC):
+            for i in range(NX):
                 signal((s - 1, hid(xs[i], y, cs[e])))
+            for i in far:
+                signal((s - 1, hid(x, ys[i], cs[e])))
 
     @pl.when(has_above)
     def _():
-        for i in range(NX):
-            for e in range(NC):
+        for e in range(NC):
+            for i in range(NX):
                 signal((s + 1, hid(xs[i], y, cs[e])))
+            for i in far:
+                signal((s + 1, hid(x, ys[i], cs[e])))
 
     for o in far:
         signal((s, hid(xs[o], y, oc)))
@@ -206,7 +227,7 @@
 
     neighbours = has_below.astype(jnp.int32) + has_above.astype(jnp.int32)
     with jax.named_scope("entry"):
-        pl.semaphore_wait(barrier, CHIPS + 2 * (NX - 1) + NX * NC * neighbours)
+        pl.semaphore_wait(barrier, CHIPS + 2 * (NX - 1) + NC * (NX + NY - 1) * neighbours)
 
     def gather_rows(t, targets):
         for i, j in targets:
@@ -241,12 +262,25 @@
                 (s, hid(xs[i], ys[j], c)),
             )
 
-    def low_cotangent():
-        l_high, l_low = split(l_f32[...])
-        r_high, r_low = split(r_f32[...])
-        l_three = jnp.concatenate([l_high, l_high, l_low], axis=0)
-        r_three = jnp.concatenate([r_high, r_low, r_high], axis=0)
-        return mm(l_three, r_three, ((0,), (0,))).astype(BF16)
+    def unpack(pieces, t):
+        for j in range(PIECES):
+            for e in range(NC):
+                z_full[e * HALF : (e + 1) * HALF, j * LANES : (j + 1) * LANES] = pieces[t, j * NC + e]
+        return z_full[...]
+
+    def total(pieces, t, base, count):
+        value = pieces[t, base]
+        for j in range(1, count):
+            value = value + pieces[t, base + j]
+        return value
+
+    def three_columns():
+        high, low = split(a_f32[...])
+        return jnp.concatenate([high, high, low], axis=0).T
+
+    def low_cotangent(columns):
+        high, low = split(z_full[...])
+        return mm(columns, jnp.concatenate([high, low, high], axis=0)).astype(BF16)
 
     gather_rows(0, chips)
     with jax.named_scope("loads"):
@@ -258,12 +292,13 @@
         l_f32[...] = l_inc[0]
         r_f32[...] = r_inc[0]
 
+    a_f32[...] = l_f32[...]
+    z_full[...] = r_f32[...]
     for t in range(TICKS):
         last = t + 1 == TICKS
         if t > 0:
-            drain(rbuf.at[t - 1, pl.ds(0, NX * NC - 1)], r_recv.at[t - 1], "r_recv")
-            for j in range(PIECES):
-                b_f32[:, j * LANES : (j + 1) * LANES] = rbuf[t - 1, j]
+            drain(rbuf.at[t - 1, pl.ds(0, 2 * (GROUP - 1))], r_recv.at[t - 1], "r_recv")
+            b_f32[...] = times(inverse, unpack(rbuf, t - 1))
         with jax.named_scope("v"):
             v = thin(b_f32[...], wi[...], ((1,), (0,)))
         if t > 0:
@@ -271,18 +306,26 @@
             @pl.when(has_above)
             def _():
                 drain(lz.at[t - 1], l_recv.at[t - 1], "l_recv")
-                l_f32[...] = lz[t - 1]
+                l_f32[...] = lz[t - 1, :, :ROWS]
+                above = lz[t - 1, :, ROWS : ROWS + RANK]
+                a_f32[...] = mm_high(above, l_f32[...], ((0,), (0,)))
+
+            @pl.when(is_top)
+            def _():
+                l_f32[...] = l_inc[t]
+                a_f32[...] = l_inc[t]
+                z_full[...] = r_inc[t]
+
+        columns = three_columns()
+        if t > 0:
+
+            @pl.when(has_above)
+            def _():
                 drain(rzbuf.at[t - 1], rz_recv.at[t - 1], "rz_recv")
-                for j in range(PIECES):
-                    r_f32[:, j * LANES : (j + 1) * LANES] = rzbuf[t - 1, j]
-
-            @pl.when(is_top)
-            def _():
-                l_f32[...] = l_inc[t]
-                r_f32[...] = r_inc[t]
+                unpack(rzbuf, t - 1)
 
         with jax.named_scope("upward"):
-            upward = mm(low_cotangent(), wo[...], ((1,), (1,)))
+            upward = mm(low_cotangent(columns), wo[...], ((1,), (1,)))
             if t > 0:
                 hg[...] = upward.astype(BF16) * mask[...]
             else:
@@ -293,29 +336,54 @@
             hg[...] = hg[...] * mask[...]
         with jax.named_scope("p_part"):
             p_part = thin(v, hg[...], ((1,), (1,)))
-            ps[t, 0] = p_part[:, :LANES]
-            ps[t, 1] = p_part[:, LANES:]
+            for e in range(NC):
+                for k in range(2):
+                    ps[t, e, k] = p_part[k * HALF : (k + 1) * HALF, e * LANES : (e + 1) * LANES]
         for o, e in group:
             send(
-                ps.at[t, cs[e]],
+                ps.at[t, cs[e], 0],
                 pbuf1.at[t, g1],
                 p1_send.at[t],
                 p1_recv.at[t],
                 (s, hid(xs[o], y, cs[e])),
             )
-        pbuf1[t, g1] = ps[t, c]
+            send(
+                ps.at[t, cs[e], 1],
+                pbuf1.at[t, GROUP + g2],
+                p1_send.at[t],
+                p1_recv.at[t],
+                (s, hid(x, ys[o], cs[e])),
+            )
+        pbuf1[t, g1] = ps[t, c, 0]
+        pbuf1[t, GROUP + g2] = ps[t, c, 1]
         if not last:
             gather_rows(t + 1, chips[:5])
+        if t > 0:
+
+            @pl.when(has_above)
+            def _():
+                above = lz[t - 1, :, ROWS : ROWS + RANK]
+                r_f32[...] = times(above, z_full[...])
+
+            @pl.when(is_top)
+            def _():
+                r_f32[...] = z_full[...]
+
         with jax.named_scope("p_cot"):
             cross = mm_high(b_f32[...], r_f32[...], ((1,), (1,)))
             p_cot = mm_high(cross, l_f32[...])
+        with jax.named_scope("merged"):
+            partial = mm(hg[...], wi[...], ((1,), (1,)))
+            if last:
+                mfull[...] = partial
+            partial_high, partial_low = split(partial)
+            m_high[...] = partial_high
+            m_low[...] = partial_low
         if last:
-            with jax.named_scope("merged"):
-                mfull[...] = mm(hg[...], wi[...], ((1,), (1,)))
-                for k in range(CHIPS):
-                    for e in range(NC):
-                        base = (k * NC + e) * OWN
-                        msend[e, k] = mfull[base : base + OWN, :].astype(BF16)
+            for k in range(CHIPS):
+                for e in range(NC):
+                    base = (k * NC + e) * OWN
+                    msend[e, k] = mfull[base : base + OWN, :].astype(BF16)
             send(
                 msend.at[oc],
                 mpair,
@@ -323,20 +391,28 @@
                 m_recv.at[0],
                 (s, hid(x, y, oc)),
             )
-        drain(pbuf1.at[t, pl.ds(0, NX * NC - 1)], p1_recv.at[t], "p1_recv")
-        p_sum = pbuf1[t, 0]
-        for j in range(1, NX * NC):
-            p_sum = p_sum + pbuf1[t, j]
-        ps1[t] = p_sum
+        drain(pbuf1.at[t, pl.ds(0, 2 * (GROUP - 1))], p1_recv.at[t], "p1_recv")
+        first = total(pbuf1, t, 0, GROUP)
+        second = total(pbuf1, t, GROUP, GROUP)
+        ps1[t, 0] = first
+        ps1[t, 1] = second
         for o, e in group:
             send(
-                ps1.at[t],
+                ps1.at[t, 0],
                 pbuf2.at[t, c * NY + y],
                 p2_send.at[t],
                 p2_recv.at[t],
                 (s, hid(x, ys[o], cs[e])),
             )
-        pbuf2[t, c * NY + y] = p_sum
+            send(
+                ps1.at[t, 1],
+                pbuf2.at[t, GROUP + c * NX + x],
+                p2_send.at[t],
+                p2_recv.at[t],
+                (s, hid(xs[o], y, cs[e])),
+            )
+        pbuf2[t, c * NY + y] = first
+        pbuf2[t, GROUP + c * NX + x] = second
         if last:
             drain(mpair, m_recv.at[0], "m_recv")
             with jax.named_scope("mpart"):
@@ -345,29 +421,35 @@
             mbuf[chip] = mpart[chip]
         else:
             gather_rows(t + 1, chips[5:10])
-        drain(pbuf2.at[t, pl.ds(0, NY * NC - 1)], p2_recv.at[t], "p2_recv")
+        drain(pbuf2.at[t, pl.ds(0, 2 * (GROUP - 1))], p2_recv.at[t], "p2_recv")
         with jax.named_scope("z_part"):
             halves = []
-            for e in range(NC):
-                half = pbuf2[t, e * NY]
-                for j in range(1, NY):
-                    half = half + pbuf2[t, e * NY + j]
-                halves.append(half)
-            projected = jnp.concatenate(halves, axis=1) + p_cot
-            y_part = thin(projected, hg[...], ((1,), (0,)))
-            z_part = thin(y_part, wi[...], ((1,), (1,)))
+            for k in range(2):
+                two = [total(pbuf2, t, k * GROUP + e * NY, NY) for e in range(NC)]
+                halves.append(jnp.concatenate(two, axis=1))
+            projected = jnp.concatenate(halves, axis=0) + p_cot
+            z_part = thin(projected, m_high[...], ((1,), (0,)))
+            z_part = z_part + mm(projected.astype(BF16), m_low[...])
             for j in range(PIECES):
-                zs[t, j] = z_part[:, j * LANES : (j + 1) * LANES]
+                for e in range(NC):
+                    zs[t, j * NC + e] = z_part[e * HALF : (e + 1) * HALF, j * LANES : (j + 1) * LANES]
         for o, e in group:
-            j = xs[o] * NC + cs[e]
-            send(
-                zs.at[t, j],
+            send(
+                zs.at[t, xs[o] * NC + cs[e]],
                 zbuf1.at[t, g1],
                 z1_send.at[t],
                 z1_recv.at[t],
                 (s, hid(xs[o], y, cs[e])),
             )
+            send(
+                zs.at[t, GROUP + ys[o] * NC + cs[e]],
+                zbuf1.at[t, GROUP + g2],
+                z1_send.at[t],
+                z1_recv.at[t],
+                (s, hid(x, ys[o], cs[e])),
+            )
         zbuf1[t, g1] = zs[t, g1]
+        zbuf1[t, GROUP + g2] = zs[t, GROUP + g2]
         if last:
             scatter_merged(chips[5:10])
         else:
@@ -380,7 +462,8 @@
                 rows_f32[...] = new_left.T
                 left_out[...] = rows_f32[pl.ds(pl.multiple_of(h * OWN, OWN), OWN), :]
             else:
-                ls[t] = new_left
+                ls[t, :, :ROWS] = new_left
+                ls[t, :, ROWS:] = jnp.concatenate([inverse, jnp.zeros((RANK, LANES - RANK), F32)], axis=1)
         if not last:
 
             @pl.when(has_below)
@@ -389,21 +472,33 @@
 
         with jax.named_scope("z_cot"):
             mix = mm_high(projected, l_f32[...], ((1,), (1,)))
-            z_cot = mm_high(mix, r_f32[:, pl.ds(pl.multiple_of(g1 * LANES, LANES), LANES)])
-        drain(zbuf1.at[t, pl.ds(0, NX * NC - 1)], z1_recv.at[t], "z1_recv")
-        z_sum = zbuf1[t, 0]
-        for j in range(1, NX * NC):
-            z_sum = z_sum + zbuf1[t, j]
-        zs1[t] = z_sum
+            for k, place in enumerate((x, NX + y)):
+                lanes = pl.ds(pl.multiple_of(place * LANES, LANES), LANES)
+                z_cot = mm_high(mix, r_f32[:, lanes])
+                for e in range(NC):
+                    zc[k, e] = z_cot[e * HALF : (e + 1) * HALF, :]
+        drain(zbuf1.at[t, pl.ds(0, 2 * (GROUP - 1))], z1_recv.at[t], "z1_recv")
+        first = total(zbuf1, t, 0, GROUP)
+        second = total(zbuf1, t, GROUP, GROUP)
+        zs1[t, 0] = first
+        zs1[t, 1] = second
         for o in far:
             send(
-                zs1.at[t],
+                zs1.at[t, 0],
                 zbuf2.at[t, y],
                 z2_send.at[t],
                 z2_recv.at[t],
                 (s, hid(x, ys[o], c)),
             )
-        zbuf2[t, y] = z_sum
+            send(
+                zs1.at[t, 1],
+                zbuf2.at[t, NY + x],
+                z2_send.at[t],
+                z2_recv.at[t],
+                (s, hid(xs[o], y, c)),
+            )
+        zbuf2[t, y] = first
+        zbuf2[t, NY + x] = second
         if not last:
             share_rows(t + 1)
             make_mask(t + 1)
@@ -413,56 +508,58 @@
                 rows_f32[...] = l_f32[...].T
                 own_left = rows_f32[pl.ds(pl.multiple_of(h * OWN, OWN), OWN), :]
                 merged = mm_high(own_left, r_f32[...])
-        drain(zbuf2.at[t, pl.ds(0, NY - 1)], z2_recv.at[t], "z2_recv")
+        drain(zbuf2.at[t, pl.ds(0, 2 * (NY - 1))], z2_recv.at[t], "z2_recv")
         with jax.named_scope("r_piece"):
-            z_piece = z_cot
-            for j in range(NY):
-                z_piece = z_piece + zbuf2[t, j]
-            r_piece = mm_high(inverse, z_piece)
-            rp[t] = r_piece
+            first = total(zbuf2, t, 0, NY) + zc[0, c]
+            second = total(zbuf2, t, NY, NX) + zc[1, c]
+            zp[t, 0] = first
+            zp[t, 1] = second
+        slots = (g1, GROUP + g2)
         if not last:
 
             @pl.when(has_below)
             def _():
                 for i in (2, 1, 3, 0):
                     for e in range(NC):
-                        send(
-                            rp.at[t],
-                            rzbuf.at[t, g1],
-                            rz_send.at[t],
-                            rz_recv.at[t],
-                            (s - 1, hid(xs[i], y, cs[e])),
-                        )
+                        for k, place in enumerate((hid(xs[i], y, cs[e]), hid(x, ys[i], cs[e]))):
+                            send(
+                                zp.at[t, k],
+                                rzbuf.at[t, slots[k]],
+                                rz_send.at[t],
+                                rz_recv.at[t],
+                                (s - 1, place),
+                            )
 
         for o, e in group:
-            send(
-                rp.at[t],
-                rbuf.at[t, g1],
-                r_send.at[t],
-                r_recv.at[t],
-                (s, hid(xs[o], y, cs[e])),
-            )
-        rbuf[t, g1] = r_piece
+            for k, place in enumerate((hid(xs[o], y, cs[e]), hid(x, ys[o], cs[e]))):
+                send(
+                    zp.at[t, k],
+                    rbuf.at[t, slots[k]],
+                    r_send.at[t],
+                    r_recv.at[t],
+                    (s, place),
+                )
+        rbuf[t, g1] = first
+        rbuf[t, GROUP + g2] = second
 
     t = TICKS - 1
     drain(mbuf.at[pl.ds(0, CHIPS - 1)], m_recv.at[1], "m_recv")
     for k in range(CHIPS):
         merged = merged + mbuf[k].astype(F32)
     grads_out[...] = merged
-    drain(rbuf.at[t, pl.ds(0, NX * NC - 1)], r_recv.at[t], "r_recv")
-    for j in range(PIECES):
-        right_out[:, j * LANES : (j + 1) * LANES] = rbuf[t, j]
+    drain(rbuf.at[t, pl.ds(0, 2 * (GROUP - 1))], r_recv.at[t], "r_recv")
+    right_out[...] = times(inverse, unpack(rbuf, t))
 
     drain(msend.at[0], m_send.at[0])
     drain(mbuf.at[pl.ds(0, CHIPS - 1)], m_send.at[1])
     for t in range(TICKS):
         drain(x_full.at[t, pl.ds(0, CHIPS - 1), 0], ag_send.at[t])
         drain(x_full.at[t, :, 0], agp_send.at[t])
-        drain(pbuf1.at[t, pl.ds(0, NX * NC - 1)], p1_send.at[t])
-        drain(pbuf2.at[t, pl.ds(0, NY * NC - 1)], p2_send.at[t])
-        drain(zbuf1.at[t, pl.ds(0, NX * NC - 1)], z1_send.at[t])
-        drain(zbuf2.at[t, pl.ds(0, NY - 1)], z2_send.at[t])
-        drain(rbuf.at[t, pl.ds(0, NX * NC - 1)], r_send.at[t])
+        drain(pbuf1.at[t, pl.ds(0, 2 * (GROUP - 1))], p1_send.at[t])
+        drain(pbuf2.at[t, pl.ds(0, 2 * (GROUP - 1))], p2_send.at[t])
+        drain(zbuf1.at[t, pl.ds(0, 2 * (GROUP - 1))], z1_send.at[t])
+        drain(zbuf2.at[t, pl.ds(0, 2 * (NY - 1))], z2_send.at[t])
+        drain(rbuf.at[t, pl.ds(0, 2 * (GROUP - 1))], r_send.at[t])
         if t + 1 < TICKS:
 
             @pl.when(has_below)
@@ -488,7 +585,6 @@
     incoming_right,
 ):
     width = w_in.shape[2]
-    group = NX * NC
     dma = pltpu.SemaphoreType.DMA
     anywhere = pl.BlockSpec(memory_space=pltpu.MemorySpace.HBM)
     inside = pl.BlockSpec(memory_space=pltpu.VMEM)
@@ -513,19 +609,24 @@
             pltpu.VMEM((RANK, D), F32),
             pltpu.VMEM((TICKS, RANK, ROWS), F32),
             pltpu.VMEM((TICKS, RANK, D), F32),
-            pltpu.VMEM((TICKS, NC, RANK, LANES), F32),
-            pltpu.VMEM((TICKS, group, RANK, LANES), F32),
-            pltpu.VMEM((TICKS, RANK, LANES), F32),
-            pltpu.VMEM((TICKS, NC * NY, RANK, LANES), F32),
-            pltpu.VMEM((TICKS, PIECES, RANK, LANES), F32),
-            pltpu.VMEM((TICKS, group, RANK, LANES), F32),
-            pltpu.VMEM((TICKS, RANK, LANES), F32),
-            pltpu.VMEM((TICKS, NY, RANK, LANES), F32),
-            pltpu.VMEM((TICKS, RANK, LANES), F32),
-            pltpu.VMEM((TICKS, group, RANK, LANES), F32),
-            pltpu.VMEM((TICKS, group, RANK, LANES), F32),
-            pltpu.VMEM((TICKS, RANK, ROWS), F32),
-            pltpu.VMEM((TICKS, RANK, ROWS), F32),
+            pltpu.VMEM((TICKS, NC, 2, HALF, LANES), F32),
+            pltpu.VMEM((TICKS, 2 * GROUP, HALF, LANES), F32),
+            pltpu.VMEM((TICKS, 2, HALF, LANES), F32),
+            pltpu.VMEM((TICKS, 2 * GROUP, HALF, LANES), F32),
+            pltpu.VMEM((TICKS, 2 * GROUP, HALF, LANES), F32),
+            pltpu.VMEM((TICKS, 2 * GROUP, HALF, LANES), F32),
+            pltpu.VMEM((TICKS, 2, HALF, LANES), F32),
+            pltpu.VMEM((TICKS, NY + NX, HALF, LANES), F32),
+            pltpu.VMEM((2, NC, HALF, LANES), F32),
+            pltpu.VMEM((TICKS, 2, HALF, LANES), F32),
+            pltpu.VMEM((RANK, D), F32),
+            pltpu.VMEM((RANK, ROWS), F32),
+            pltpu.VMEM((ROWS, D), BF16),
+            pltpu.VMEM((ROWS, D), BF16),
+            pltpu.VMEM((TICKS, 2 * GROUP, HALF, LANES), F32),
+            pltpu.VMEM((TICKS, 2 * GROUP, HALF, LANES), F32),
+            pltpu.VMEM((TICKS, RANK, ROWS + LANES), F32),
+            pltpu.VMEM((TICKS, RANK, ROWS + LANES), F32),
             pltpu.VMEM((ROWS, RANK), F32),
             pltpu.VMEM((ROWS, D), F32),
             pltpu.VMEM((NC, CHIPS, OWN, D), BF16),

time: 86.9 us -> 84.6 us (0.974)
  Pallas kernels: 86 us -> 83.7 us
    pallas_call x1, Pallas kernels: 84.5 us -> 82.1 us  [body(): pl.pallas_call(kernel, out_shape=results, in_specs=[anywhere] * 8, out_sp...]
where the time goes in v2:
time: 84.6 us; the launch traced here: 84.3 us
  Pallas kernels  83.7 us (99%)
    pallas_call x1, Pallas kernels, body(): pl.pallas_call(kernel, out_shape=results, in_specs=[anywhere] * 8, out_sp...  82.1 us

profile of v2, /device:TPU:1, one launch (start us, length us, event | category | flops | bytes accessed | tf_op | source)
XLA Modules:
  0.0 84.3 jit_solution(15199510977384402457)
XLA Ops:
  0.6 82.1 %shard_map.103 = (f32[8,1024]{1,0:T(8,128)}, f32[8,16]{1,0:T(8,128)}, f32[16,1024]{1,0:T(8,128)}) custom-call(bf16[3,8,1024]{2,1,0:T(8,128)(2,1)} %bitcast.24, bf16[1024,1024]{1,0:T(8,128)(2,1)} %bitcast.19, bf16[1024,1024]{1,0:T(8,128)(2,1)} %bitcast.20, f32[16,1024]{1,0:T(8,128)} %bitcast.22, f32[16,256]{1,0:T(8,128)} %bitcast.26, f32[16,1024]{1,0:T(8,128)} %bitcast.23, ...), custom_call_target="tpu_custom_call" | custom-call | tf_op jit(solution)/shard_map/pallas_call | solution.py:596
  82.8 1.5 %shard_map.104 = (f32[8,1024]{1,0:T(8,128)}, f32[8,16]{1,0:T(8,128)}, f32[16,1024]{1,0:T(8,128)}) custom-call(f32[8,1024]{1,0:T(8,128)} %get-tuple-element.9.merged_in, f32[8,16]{1,0:T(8,128)} %get-tuple-element.10.left_in, f32[16,1024]{1,0:T(8,128)} %get-tuple-element.11.right_in), custom_call_target="tpu_custom_call" | custom-call | tf_op jit(solution)/shard_map/pallas_call | solution.py:654

commit v3 on v2

--- a/solution.py
+++ b/solution.py
@@ -595,7 +595,7 @@
     )
     found = pl.pallas_call(
         kernel,
-        out_shape=results,
+        out_shape=tuple(pltpu.VMEM(r.shape, r.dtype) for r in results),
         in_specs=[anywhere] * 8,
         out_specs=(inside, inside, inside),
         scratch_shapes=[
@@ -639,7 +639,7 @@
         + [dma((TICKS,))] * 16
         + [dma((2,))] * 2,
         compiler_params=pltpu.CompilerParams(
-            collective_id=0, has_side_effects=True, vmem_limit_bytes=67043328
+            collective_id=0, has_side_effects=True, vmem_limit_bytes=66781184
         ),
     )(
         section_inputs[0],
@@ -652,7 +652,11 @@
         jnp.swapaxes(incoming_right, 1, 2),
     )
     merged, left, right = pl.pallas_call(
-        hand_over, out_shape=results, in_specs=[inside] * 3, out_specs=(inside,) * 3
+        hand_over,
+        out_shape=results,
+        in_specs=[inside] * 3,
+        out_specs=(inside,) * 3,
+        compiler_params=pltpu.CompilerParams(vmem_limit_bytes=1024 * 1024),
     )(*found)
     return (merged[None], left[None], jnp.swapaxes(right, 0, 1)[None])
 

time: 84.6 us -> 83 us (0.981)
  Pallas kernels: 83.7 us -> 82.2 us
    pallas_call x1, Pallas kernels: 1.51 us -> 0.65 us  [body(): pl.pallas_call(hand_over, out_shape=results, in_specs=[inside] * 3, out_s...]
where the time goes in v3:
time: 83 us; the launch traced here: 82.9 us
  Pallas kernels  82.2 us (99%)
    pallas_call x1, Pallas kernels, body(): pl.pallas_call(kernel, out_shape=tuple((pltpu.VMEM(r.shape, r.dtype) for...  81.6 us

profile of v3, /device:TPU:1, one launch (start us, length us, event | category | flops | bytes accessed | tf_op | source)
XLA Modules:
  0.0 82.9 jit_solution(8371197326537756347)
XLA Ops:
  0.6 81.6 %shard_map.103 = (f32[8,1024]{1,0:T(8,128)S(1)}, f32[8,16]{1,0:T(8,128)S(1)}, f32[16,1024]{1,0:T(8,128)S(1)}) custom-call(bf16[3,8,1024]{2,1,0:T(8,128)(2,1)} %bitcast.24, bf16[1024,1024]{1,0:T(8,128)(2,1)} %bitcast.19, bf16[1024,1024]{1,0:T(8,128)(2,1)} %bitcast.20, f32[16,1024]{1,0:T(8,128)} %bitcast.22, f32[16,256]{1,0:T(8,128)} %bitcast.26, ...), custom_call_target="tpu_custom_call" | custom-call | tf_op jit(solution)/shard_map/pallas_call | solution.py:596
  82.2 0.6 shard_map.104
